TPU v7x, 256 devices: a whole 4x4x8 slice. The times are simulated.
256 devices in a mesh: tm: 32 (over z, x), region: 8 (over y, core).
Axes of the slice: x: 4, y: 4, z: 8, core: 2. Of those that a mesh axis runs over, the one named last changes fastest.
Arguments:
- start_primal: float32 [2048, 8, 3200], P('tm', 'region'), may hold values from 0 to 10, as said below
- demand: float32 [2048, 8, 3200], P('tm', 'region'), may hold values from -30 to 30
- unit_cost: float32 [8, 3200], P('region'), may hold values from -5 to 5
- build_cost: float32 [8, 128], P('region', 'tm'), may hold values from 0.5 to 2
- start_capacity: float32 [8, 128], P('region', 'tm'), may hold values from 0 to 2
- net_weights: float32 [8, 25, 3, 128, 128], P('region'), may hold values from -0.3125 to 0.3125
- net_columns: int32 [8, 25, 3], P('region'), may hold values from 0 to 24
- line_weights: float32 [8, 4, 128, 128], P('region'), may hold values from -0.25 to 0.25
- line_source: int32 [8, 4], replicated, may hold values from 0 to 7
- generator_map: int32 [8, 128], P('region'), may hold values from 0 to 127
Outputs:
- primal_final: float32 [2048, 8, 3200], P('tm', 'region')
- dual_final: float32 [2048, 8, 3200], P('tm', 'region')
- capacity_final: float32 [8, 128], P('region', 'tm')
Inputs may be any that keep to these rules, and one draw needn't show every extreme that they name: `start_primal`: Nonnegative.
All inputs are finite; a program needn't handle non-finite values.
Results may differ from a plain program's by a relative error of at most 0.0003.
Values sent between devices are 32-bit elements; how exact they have to be, the bound alone decides.
A program may use at most 64 MiB of HBM per device.

v0:
```python
import math
import jax
import jax.numpy as jnp
from jax import lax
from jax.sharding import PartitionSpec as P

ITERS = 4
HIGHEST_PRECISION = lax.Precision.HIGHEST
STEP_SCALE = 0.2
EPSILON = 1e-06


def shifted(shard, axis, by):
    devices = lax.axis_size(axis)
    pairs = [(i, i + by) for i in range(devices) if 0 <= i + by < devices]
    return lax.ppermute(shard, axis, pairs)


def network_forward(blocks, weights, columns):
    hour_count = blocks.shape[0]
    picked = jnp.take(blocks, columns.reshape(-1), axis=1)
    flat_weights = weights.reshape(-1, weights.shape[2], weights.shape[3])
    product = jnp.einsum("hpk,pkl->hpl", picked, flat_weights, precision=HIGHEST_PRECISION)
    return product.reshape(hour_count, columns.shape[0], columns.shape[1], -1).sum(axis=2)


def network_adjoint(dual_rows, weights, columns):
    hour_count = dual_rows.shape[0]
    partial_value = jnp.einsum("hil,iskl->hisk", dual_rows, weights, precision=HIGHEST_PRECISION)
    block_count = columns.shape[0]
    placing = (columns.reshape(-1)[:, None] == jnp.arange(block_count)[None, :]).astype(jnp.float32)
    stacked = partial_value.reshape(hour_count, -1, partial_value.shape[3])
    return jnp.einsum("hpk,pc->hck", stacked, placing, precision=HIGHEST_PRECISION)


def body(
    start_primal,
    demand,
    unit_cost,
    build_cost,
    start_capacity,
    net_weights,
    net_columns,
    line_weights,
    line_source,
    generator_map,
):
    hour_count, _, row_width = start_primal.shape
    block_size = net_weights.shape[3]
    block_count = row_width // block_size
    tm_count = lax.axis_size("tm")
    region_count = lax.axis_size("region")
    own_region = lax.axis_index("region")
    weights = net_weights[0]
    columns = net_columns[0]
    line_mats = line_weights[0]
    unit_rows = unit_cost.reshape(block_count, block_size)
    invest_own = start_capacity.shape[1]
    invest_all = invest_own * tm_count
    couple = 1.0 / math.sqrt(hour_count * tm_count)
    primal_count = hour_count * tm_count * region_count * row_width + region_count * invest_all
    dual_count = hour_count * tm_count * region_count * row_width
    selector = (generator_map[0][:, None] == jnp.arange(invest_all)[None, :]).astype(jnp.float32)
    line_links = (line_source[:, :, None] == jnp.arange(region_count)[None, None, :]).astype(
        jnp.float32
    )
    own_sources = lax.dynamic_index_in_dim(line_links, own_region, 0, keepdims=False)
    free_column = (jnp.arange(block_count) == 3)[None, :, None]
    free_row = (jnp.arange(block_count) < 3)[None, :, None]
    primal = start_primal.reshape(hour_count, block_count, block_size)
    target = demand.reshape(hour_count, block_count, block_size)
    dual = jnp.zeros_like(primal)
    primal_weight = jnp.float32(1.0)
    capacity, build_rows = (
        lax.all_gather(start_capacity[0], "tm", axis=0, tiled=True),
        lax.all_gather(build_cost[0], "tm", axis=0, tiled=True),
    )
    for iteration in range(ITERS):
        primal_step = STEP_SCALE / primal_weight
        dual_step = STEP_SCALE * primal_weight
        adjoint = network_adjoint(dual, weights, columns)
        after = shifted(dual[0, 0], "tm", -1)
        following = jnp.concatenate([dual[1:, 0], after[None]], axis=0)
        partial_lines = jnp.einsum(
            "hl,jkl->jhk", dual[:, 1], line_mats, precision=HIGHEST_PRECISION
        )
        line_back = lax.psum_scatter(
            jnp.einsum("jq,jhk->qhk", own_sources, partial_lines, precision=HIGHEST_PRECISION),
            "region",
            scatter_dimension=0,
            tiled=True,
        )[0]
        adjoint = adjoint.at[:, 0].add(-following).at[:, 3].add(line_back)
        column_sums = jnp.sum(dual[:, 2], axis=0)
        capacity_part = couple * jnp.dot(column_sums, selector, precision=HIGHEST_PRECISION)
        moved = primal - primal_step * (unit_rows[None] - adjoint)
        new_primal = jnp.where(free_column, moved, jnp.maximum(moved, 0.0))
        capacity_grad = lax.psum(capacity_part, "tm")
        new_capacity = jnp.maximum(capacity - primal_step * (build_rows - capacity_grad), 0.0)
        capacity_bar = 2.0 * new_capacity - capacity
        capacity_change = lax.dynamic_slice_in_dim(
            new_capacity - capacity, lax.axis_index("tm") * invest_own, invest_own, 0
        )
        primal_bar = 2.0 * new_primal - primal
        primal_local = jnp.sum((new_primal - primal) ** 2) + jnp.sum(capacity_change**2)
        if iteration + 1 < ITERS:
            primal_total = lax.psum(primal_local, ("tm", "region"))
        applied = network_forward(primal_bar, weights, columns)
        before = shifted(primal_bar[-1, 0], "tm", 1)
        earlier = jnp.concatenate([before[None], primal_bar[:-1, 0]], axis=0)
        chosen_flows = jnp.einsum(
            "jr,rhk->jhk",
            own_sources,
            lax.all_gather(primal_bar[:, 3][None], "region", axis=0, tiled=True),
            precision=HIGHEST_PRECISION,
        )
        line_flow = jnp.einsum("jhk,jkl->hl", chosen_flows, line_mats, precision=HIGHEST_PRECISION)
        picked_capacity = jnp.dot(selector, capacity_bar, precision=HIGHEST_PRECISION)
        applied = (
            applied.at[:, 0]
            .add(-earlier)
            .at[:, 1]
            .add(line_flow)
            .at[:, 2]
            .add(couple * picked_capacity[None])
        )
        moved_dual = dual + dual_step * (target - applied)
        new_dual = jnp.where(free_row, moved_dual, jnp.maximum(moved_dual, 0.0))
        if iteration + 1 < ITERS:
            dual_local = jnp.sum((new_dual - dual) ** 2)
            dual_total = lax.psum(dual_local, ("tm", "region"))
            primal_weight = jnp.sqrt(
                primal_weight
                * jnp.sqrt(primal_total / primal_count + EPSILON)
                / jnp.sqrt(dual_total / dual_count + EPSILON)
            )
        primal, dual, capacity = (new_primal, new_dual, new_capacity)
    capacity_own = lax.dynamic_slice_in_dim(
        capacity, lax.axis_index("tm") * invest_own, invest_own, 0
    )
    return (
        primal.reshape(hour_count, 1, row_width),
        dual.reshape(hour_count, 1, row_width),
        capacity_own[None],
    )


def solution(mesh):
    in_specs = (
        P("tm", "region", None),
        P("tm", "region", None),
        P("region", None),
        P("region", "tm"),
        P("region", "tm"),
        P("region", None, None, None, None),
        P("region", None, None),
        P("region", None, None, None),
        P(),
        P("region", None),
    )
    out_specs = (P("tm", "region", None), P("tm", "region", None), P("region", "tm"))
    return jax.shard_map(body, mesh=mesh, in_specs=in_specs, out_specs=out_specs, check_vma=False)
```

profile of v0, /device:TPU:1, one launch (start us, length us, event | category | flops | bytes accessed | tf_op | source)
XLA Modules:
  0.0 858.2 jit_solution(13189949462657411320)
XLA Ops:
  12.9 9.0 %fusion.6 = f32[25,64,3,128]{3,1,2,0:T(8,128)S(1)} fusion(f32[1,25,3,128,128]{4,3,2,1,0:T(8,128)} %param.57), kind=kOutput, calls=%fused_computation.10 | convolution fusion | flops 943718400 | bytes 7372800 | tf_op jit(solution)/shard_map/hil,iskl->hisk/dot_general | solution.py:29
  22.0 2.4 fusion.14
  27.1 76.9 %all-reduce.6 = (f32[128]{0:T(128)S(1)}, f32[128]{0:T(128)S(1)}, f32[128]{0:T(128)S(1)}) all-reduce(f32[128]{0:T(128)S(1)} %bitcast_dynamic-update-slice_fusion.1, f32[128]{0:T(128)S(1)} %bitcast_dynamic-update-slice_fusion, f32[128]{0:T(128)S(1)} %fusion.51), channel_id=2, replica_groups=mesh['tm'=32,'region'=8] {'tm'}, use_global_device_ids=true, to_apply=%add.1 | all-reduce | flops 384 | bytes 3072 | tf_op jit(solution)/shard_map/all_gather | solution.py:75
  106.3 3.1 reduce.43
  113.3 28.2 %all-gather.2 = f32[512,1,128]{2,1,0:T(1,128)S(1)} all-gather(f32[64,1,128]{2,1,0:T(1,128)S(1)} %bitcast.385), channel_id=4, replica_groups=mesh['tm'=32,'region'=8] {'region'}, dimensions={0}, use_global_device_ids=true | all-gather | bytes 294912 | tf_op jit(solution)/shard_map/all_gather | solution.py:114
  143.6 7.9 fusion.22
  157.0 10.5 %fusion.4 = f32[25,64,3,128]{3,1,2,0:T(8,128)} fusion(f32[1,25,3,128,128]{4,3,2,1,0:T(8,128)} %param.57, f32[64,25,128]{2,0,1:T(8,128)S(1)} %get-tuple-element.281), kind=kOutput, calls=%fused_computation.8 | convolution fusion | flops 943718400 | bytes 8192000 | tf_op jit(solution)/shard_map/hil,iskl->hisk/dot_general | solution.py:29
  167.7 55.8 %psum.73 = f32[128]{0:T(128)S(1)} all-reduce(f32[128]{0:T(128)S(1)} %fusion.49), channel_id=1, replica_groups=mesh['tm'=32,'region'=8] {'tm'}, use_global_device_ids=true, to_apply=%region_11.13 | all-reduce | flops 128 | bytes 1024 | tf_op jit(solution)/shard_map/psum | solution.py:98
  223.5 89.7 %all-reduce.5 = (f32[]{:T(128)}, f32[]{:T(128)}) all-reduce(f32[]{:T(128)S(6)} %add.249, f32[]{:T(128)} %get-tuple-element.280), channel_id=1, replica_groups=mesh['tm'=32,'region'=8] {'tm','region'}, use_global_device_ids=true, to_apply=%region_4.5 | all-reduce | flops 2 | bytes 16 | tf_op jit(solution)/shard_map/psum | solution.py:107
  317.6 4.0 fusion.12
  325.8 22.6 %reduce-scatter.7.cloned.1.call-done = f32[1,64,128]{2,1,0:T(8,128)} async-done(((f32[8,64,128]{2,1,0:T(8,128)}), f32[1,64,128]{2,1,0:T(8,128)}) %reduce-scatter.7.cloned.1.call-update) | async-done | bytes 32784 | tf_op jit(solution)/shard_map/reduce_scatter | solution.py:87
  354.9 2.8 collective-permute-start.3
  357.8 16.1 %all-gather.3 = f32[512,1,128]{2,1,0:T(1,128)S(1)} all-gather(f32[64,1,128]{2,1,0:T(1,128)S(1)} %bitcast.383), channel_id=5, replica_groups=mesh['tm'=32,'region'=8] {'region'}, dimensions={0}, use_global_device_ids=true | all-gather | bytes 294912 | tf_op jit(solution)/shard_map/all_gather | solution.py:114
  373.9 7.9 fusion.20
  387.2 10.5 %fusion.2 = f32[25,64,3,128]{3,1,2,0:T(8,128)} fusion(f32[1,25,3,128,128]{4,3,2,1,0:T(8,128)} %param.57, f32[64,25,128]{2,0,1:T(8,128)S(1)} %get-tuple-element.275), kind=kOutput, calls=%fused_computation.6 | convolution fusion | flops 943718400 | bytes 8192000 | tf_op jit(solution)/shard_map/hil,iskl->hisk/dot_general | solution.py:29
  397.9 59.1 %psum.76 = f32[128]{0:T(128)S(1)} all-reduce(f32[128]{0:T(128)S(1)} %fusion.47), channel_id=1, replica_groups=mesh['tm'=32,'region'=8] {'tm'}, use_global_device_ids=true, to_apply=%region_20.22 | all-reduce | flops 128 | bytes 1024 | tf_op jit(solution)/shard_map/psum | solution.py:98
  457.0 86.0 %all-reduce.4 = (f32[]{:T(128)}, f32[]{:T(128)}) all-reduce(f32[]{:T(128)S(6)} %add.257, f32[]{:T(128)} %get-tuple-element.274), channel_id=1, replica_groups=mesh['tm'=32,'region'=8] {'tm','region'}, use_global_device_ids=true, to_apply=%region_13.15 | all-reduce | flops 2 | bytes 16 | tf_op jit(solution)/shard_map/psum | solution.py:107
  547.2 4.0 fusion.10
  555.4 23.9 %reduce-scatter.9.cloned.1.call-done = f32[1,64,128]{2,1,0:T(8,128)} async-done(((f32[8,64,128]{2,1,0:T(8,128)}), f32[1,64,128]{2,1,0:T(8,128)}) %reduce-scatter.9.cloned.1.call-update) | async-done | bytes 32784 | tf_op jit(solution)/shard_map/reduce_scatter | solution.py:87
  580.7 2.2 multiply_reduce_fusion.1
  585.1 2.8 collective-permute-start.5
  587.9 16.1 %all-gather.4 = f32[512,1,128]{2,1,0:T(1,128)S(1)} all-gather(f32[64,1,128]{2,1,0:T(1,128)S(1)} %bitcast.384), channel_id=6, replica_groups=mesh['tm'=32,'region'=8] {'region'}, dimensions={0}, use_global_device_ids=true | all-gather | bytes 294912 | tf_op jit(solution)/shard_map/all_gather | solution.py:114
  604.0 7.9 fusion.18
  618.5 10.5 %fusion = f32[25,64,3,128]{3,1,2,0:T(8,128)} fusion(f32[1,25,3,128,128]{4,3,2,1,0:T(8,128)} %param.57, f32[64,25,128]{2,0,1:T(8,128)S(1)} %get-tuple-element.271), kind=kOutput, calls=%fused_computation.4 | convolution fusion | flops 943718400 | bytes 8192000 | tf_op jit(solution)/shard_map/hil,iskl->hisk/dot_general | solution.py:29
  629.2 59.1 %psum.79 = f32[128]{0:T(128)S(1)} all-reduce(f32[128]{0:T(128)S(1)} %fusion.45), channel_id=1, replica_groups=mesh['tm'=32,'region'=8] {'tm'}, use_global_device_ids=true, to_apply=%region_29.31 | all-reduce | flops 128 | bytes 1024 | tf_op jit(solution)/shard_map/psum | solution.py:98
  688.3 86.0 %all-reduce.3 = (f32[]{:T(128)}, f32[]{:T(128)}) all-reduce(f32[]{:T(128)S(6)} %add.266, f32[]{:T(128)} %get-tuple-element.270), channel_id=1, replica_groups=mesh['tm'=32,'region'=8] {'tm','region'}, use_global_device_ids=true, to_apply=%region_22.24 | all-reduce | flops 2 | bytes 16 | tf_op jit(solution)/shard_map/psum | solution.py:107
  778.5 4.0 fusion.8
  786.6 24.2 %reduce-scatter.11.cloned.1.call-done = f32[1,64,128]{2,1,0:T(8,128)} async-done(((f32[8,64,128]{2,1,0:T(8,128)}), f32[1,64,128]{2,1,0:T(8,128)}) %reduce-scatter.11.cloned.1.call-update) | async-done | bytes 32784 | tf_op jit(solution)/shard_map/reduce_scatter | solution.py:87
  812.2 2.7 multiply_subtract_fusion
  817.0 2.8 collective-permute-start.7
  819.9 16.1 %all-gather.5 = f32[512,1,128]{2,1,0:T(1,128)S(1)} all-gather(f32[64,1,128]{2,1,0:T(1,128)S(1)} %bitcast.382), channel_id=7, replica_groups=mesh['tm'=32,'region'=8] {'region'}, dimensions={0}, use_global_device_ids=true | all-gather | bytes 294912 | tf_op jit(solution)/shard_map/all_gather | solution.py:114
  836.0 8.0 fusion.16
  (174 shorter events, 71.9 us)
Async XLA Ops:
  7.2 97.1 %copy-start = (f32[64,1,3200]{2,1,0:T(1,128)S(1)}, f32[64,1,3200]{2,1,0:T(1,128)}, u32[]{:S(2)}) copy-start(f32[64,1,3200]{2,1,0:T(1,128)} %param.53) | copy-start | bytes 2457604
  7.2 102.9 %reduce-scatter.5.cloned.1.call-start = ((), (), s32[]{:S(2)}) async-start(), calls=%async_computation.4 | async-start | bytes 294912 | tf_op jit(solution)/shard_map/reduce_scatter | solution.py:87
  7.2 102.8 %collective-permute-start = (f32[128]{0:T(128)S(1)}, f32[128]{0:T(128)S(1)}, u32[]{:S(2)}, u32[]{:S(2)}) collective-permute-start(f32[128]{0:T(128)S(1)} %broadcast.305), channel_id=1, source_target_pairs={{8,0},{16,8},{24,16},{32,24},{40,32},{48,40},{56,48},{64,56},{72,6... | collective-permute-start | bytes 1544 | tf_op jit(solution)/shard_map/ppermute | solution.py:16
  12.0 336.4 %reduce-scatter.7.cloned.1.call-start = ((), (), s32[]{:S(2)}) async-start(), calls=%async_computation.5 | async-start | bytes 294912 | tf_op jit(solution)/shard_map/reduce_scatter | solution.py:87
  24.4 1.0 copy-start.14
  24.4 1.3 copy-start.16
  24.4 2.5 copy-start.12
  24.4 2.6 copy-start.13
  24.4 79.8 %copy-start.11 = (f32[1,3200]{1,0:T(1,128)S(1)}, f32[1,3200]{1,0:T(1,128)}, u32[]{:S(2)}) copy-start(f32[1,3200]{1,0:T(1,128)} %param.54) | copy-start | bytes 38404
  112.0 43.3 %collective-permute-start.1 = (f32[128]{0:T(128)S(1)}, f32[128]{0:T(128)S(1)}, u32[]{:S(2)}, u32[]{:S(2)}) collective-permute-start(f32[128]{0:T(128)S(1)} %slice_bitcast_fusion.16), channel_id=1, source_target_pairs={{0,8},{8,16},{16,24},{24,32},{32,40},{40,48},{48,56},{56,64},{64,7... | collective-permute-start | bytes 1544 | tf_op jit(solution)/shard_map/ppermute | solution.py:16
  151.5 3.8 copy-start.2
  156.6 10.9 %copy-start.8 = (f32[64,25,128]{2,0,1:T(8,128)}, f32[64,25,128]{2,0,1:T(8,128)S(1)}, u32[]{:S(2)}) copy-start(f32[64,25,128]{2,0,1:T(8,128)S(1)} %get-tuple-element.281) | copy-start | bytes 2457604
  167.7 153.9 %copy-start.15 = (s32[1,128]{1,0:T(1,128)S(1)}, s32[1,128]{1,0:T(1,128)}, u32[]{:S(2)}) copy-start(s32[1,128]{1,0:T(1,128)} %param.61) | copy-start | bytes 1540
  314.6 10.5 %collective-permute-start.2 = (f32[128]{0:T(128)S(1)}, f32[128]{0:T(128)S(1)}, u32[]{:S(2)}, u32[]{:S(2)}) collective-permute-start(f32[128]{0:T(128)S(1)} %slice_bitcast_fusion.15), channel_id=1, source_target_pairs={{8,0},{16,8},{24,16},{32,24},{40,32},{48,40},{56,48},{64,56},{72,6... | collective-permute-start | bytes 1544 | tf_op jit(solution)/shard_map/ppermute | solution.py:16
  317.1 262.2 %reduce-scatter.9.cloned.1.call-start = ((), (), s32[]{:S(2)}) async-start(), calls=%async_computation.6 | async-start | bytes 294912 | tf_op jit(solution)/shard_map/reduce_scatter | solution.py:87
  351.9 0.9 copy-start.3
  354.9 30.4 %collective-permute-start.3 = (f32[128]{0:T(128)S(1)}, f32[128]{0:T(128)S(1)}, u32[]{:S(2)}, u32[]{:S(2)}) collective-permute-start(f32[128]{0:T(128)S(1)} %slice_bitcast_fusion.14), channel_id=1, source_target_pairs={{0,8},{8,16},{16,24},{24,32},{32,40},{40,48},{48,56},{56,64},{64,7... | collective-permute-start | bytes 1544 | tf_op jit(solution)/shard_map/ppermute | solution.py:16
  381.8 4.0 copy-start.9
  386.8 10.9 %copy-start.7 = (f32[64,25,128]{2,0,1:T(8,128)}, f32[64,25,128]{2,0,1:T(8,128)S(1)}, u32[]{:S(2)}) copy-start(f32[64,25,128]{2,0,1:T(8,128)S(1)} %get-tuple-element.275) | copy-start | bytes 2457604
  544.5 10.3 %collective-permute-start.4 = (f32[128]{0:T(128)S(1)}, f32[128]{0:T(128)S(1)}, u32[]{:S(2)}, u32[]{:S(2)}) collective-permute-start(f32[128]{0:T(128)S(1)} %slice_bitcast_fusion.13), channel_id=1, source_target_pairs={{8,0},{16,8},{24,16},{32,24},{40,32},{48,40},{56,48},{64,56},{72,6... | collective-permute-start | bytes 1544 | tf_op jit(solution)/shard_map/ppermute | solution.py:16
  547.0 263.9 %reduce-scatter.11.cloned.1.call-start = ((), (), s32[]{:S(2)}) async-start(), calls=%async_computation.7 | async-start | bytes 294912 | tf_op jit(solution)/shard_map/reduce_scatter | solution.py:87
  551.2 29.5 %copy-start.4 = (f32[64,25,128]{2,0,1:T(8,128)S(1)}, f32[64,25,128]{2,0,1:T(8,128)}, u32[]{:S(2)}) copy-start(f32[64,25,128]{2,0,1:T(8,128)} %copy-done.3) | copy-start | bytes 2457604
  585.1 30.5 %collective-permute-start.5 = (f32[128]{0:T(128)S(1)}, f32[128]{0:T(128)S(1)}, u32[]{:S(2)}, u32[]{:S(2)}) collective-permute-start(f32[128]{0:T(128)S(1)} %slice_bitcast_fusion.12), channel_id=1, source_target_pairs={{0,8},{8,16},{16,24},{24,32},{32,40},{40,48},{48,56},{56,64},{64,7... | collective-permute-start | bytes 1544 | tf_op jit(solution)/shard_map/ppermute | solution.py:16
  618.1 10.9 %copy-start.5 = (f32[64,25,128]{2,0,1:T(8,128)}, f32[64,25,128]{2,0,1:T(8,128)S(1)}, u32[]{:S(2)}) copy-start(f32[64,25,128]{2,0,1:T(8,128)S(1)} %get-tuple-element.271) | copy-start | bytes 2457604
  775.8 10.2 %collective-permute-start.6 = (f32[128]{0:T(128)S(1)}, f32[128]{0:T(128)S(1)}, u32[]{:S(2)}, u32[]{:S(2)}) collective-permute-start(f32[128]{0:T(128)S(1)} %slice_bitcast_fusion.11), channel_id=1, source_target_pairs={{8,0},{16,8},{24,16},{32,24},{40,32},{48,40},{56,48},{64,56},{72,6... | collective-permute-start | bytes 1544 | tf_op jit(solution)/shard_map/ppermute | solution.py:16
  817.0 31.6 %collective-permute-start.7 = (f32[128]{0:T(128)S(1)}, f32[128]{0:T(128)S(1)}, u32[]{:S(2)}, u32[]{:S(2)}) collective-permute-start(f32[128]{0:T(128)S(1)} %slice_bitcast_fusion.10), channel_id=1, source_target_pairs={{0,8},{8,16},{16,24},{24,32},{32,40},{40,48},{48,56},{56,64},{64,7... | collective-permute-start | bytes 1544 | tf_op jit(solution)/shard_map/ppermute | solution.py:16
  836.0 8.4 copy-start.10
  844.9 4.1 copy-start.6
  848.9 2.4 copy-start.1
Sparse Core Ops, SparseCore 0:
  12.1 36.2 reduce-scatter.4
  317.2 31.0 reduce-scatter.6
  547.1 32.1 reduce-scatter.8
  778.6 32.1 reduce-scatter.10
where the time goes:
time: 867 us; the launch traced here: 858 us
  blocking collectives  589 us (68%)
  matrix products  94.9 us (11%)
  waiting for transfers between devices  70.8 us (8%)
  other arithmetic  35 us (4%)
  local copies, waits for them, and re-layouts  28.8 us (3%)
  between operations  23.7 us (3%)
  starting transfers between devices  16 us (2%)
    psum x3, blocking collectives, body(): primal_total = lax.psum(primal_local, ('tm', 'region'))  262 us
    psum x3, blocking collectives, body(): capacity_grad = lax.psum(capacity_part, 'tm')  174 us
    all_gather x1, blocking collectives, body(): lax.all_gather(start_capacity[0], 'tm', axis=0, tiled=True)  76.9 us
    all_gather x4, blocking collectives, body(): lax.all_gather(primal_bar[:, 3][None], 'region', axis=0, tiled=True)  76.5 us
    reduce_scatter x4, waiting for transfers between devices, body(): lax.psum_scatter(jnp.einsum('jq,jhk->qhk', own_sources, partial_lines, pr...  70.7 us
    dot_general x4, matrix products, network_adjoint(): jnp.einsum('hil,iskl->hisk', dual_rows, weights, precision=HIGHEST_PRECIS...  40.4 us
    dot_general x4, matrix products, network_forward(): jnp.einsum('hpk,pkl->hpl', picked, flat_weights, precision=HIGHEST_PRECIS...  31.7 us
  transfers between devices with their start and end apart: 12, of which 3 were waited for; matrix products, arithmetic and copies ran while one was open for 11% of the time, Pallas kernels for 0%

commit v1 on v0

--- a/solution.py
+++ b/solution.py
@@ -3,6 +3,7 @@
 import jax.numpy as jnp
 from jax import lax
 from jax.sharding import PartitionSpec as P
+from jax.lax import axis_size, ppermute
 
 ITERS = 4
 HIGHEST_PRECISION = lax.Precision.HIGHEST
@@ -95,7 +96,21 @@
         capacity_part = couple * jnp.dot(column_sums, selector, precision=HIGHEST_PRECISION)
         moved = primal - primal_step * (unit_rows[None] - adjoint)
         new_primal = jnp.where(free_column, moved, jnp.maximum(moved, 0.0))
-        capacity_grad = lax.psum(capacity_part, "tm")
+
+        def return_all_array_up(piece_in, axis_key):
+            current_value, new = (piece_in, 0)
+            n_lanes = axis_size(axis_key)
+            while 1 << new < n_lanes:
+                h_now = ppermute(
+                    current_value,
+                    axis_name=axis_key,
+                    perm=[(idx, idx ^ 1 << new) for idx in range(n_lanes)],
+                )
+                current_value = current_value + h_now
+                new = new + 1
+            return current_value
+
+        capacity_grad = return_all_array_up(capacity_part, axis_key="tm")
         new_capacity = jnp.maximum(capacity - primal_step * (build_rows - capacity_grad), 0.0)
         capacity_bar = 2.0 * new_capacity - capacity
         capacity_change = lax.dynamic_slice_in_dim(

time: 867 us -> 699 us (0.81)
  blocking collectives: 589 us -> 375 us
  starting transfers between devices: 16 us -> 59 us
    psum x3 -> x0, blocking collectives: 174 us -> none  [body(): capacity_grad = lax.psum(capacity_part, 'tm')]
    ppermute x0 -> x20, starting transfers between devices: none -> 43.7 us  [return_all_array_up(): ppermute(current_value, axis_name=axis_key, perm=[(idx, idx ^ 1 << new) f...]
    psum x3, blocking collectives: 262 us -> 233 us  [body(): primal_total = lax.psum(primal_local, ('tm', 'region'))]
    all_gather x1, blocking collectives: 76.9 us -> 61.3 us  [body(): lax.all_gather(start_capacity[0], 'tm', axis=0, tiled=True)]
    ppermute x0 -> x20, waiting for transfers between devices: none -> 13.7 us  [return_all_array_up(): ppermute(current_value, axis_name=axis_key, perm=[(idx, idx ^ 1 << new) f...]
    reduce_scatter x4, waiting for transfers between devices: 70.7 us -> 60.6 us  [body(): lax.psum_scatter(jnp.einsum('jq,jhk->qhk', own_sources, partial_lines, pr...]
  transfers between devices with their start and end apart: 12 -> 32, of which waited for: 3 -> 10; matrix products, arithmetic and copies ran while one was open for 11% -> 14% of each run, Pallas kernels for 0% -> 0%
where the time goes in v1:
time: 699 us; the launch traced here: 688 us
  blocking collectives  375 us (54%)
  matrix products  87.4 us (13%)
  waiting for transfers between devices  74.3 us (11%)
  starting transfers between devices  59 us (8%)
  other arithmetic  37.3 us (5%)
  local copies, waits for them, and re-layouts  31.3 us (4%)
  between operations  23.8 us (3%)
    psum x3, blocking collectives, body(): primal_total = lax.psum(primal_local, ('tm', 'region'))  233 us
    all_gather x4, blocking collectives, body(): lax.all_gather(primal_bar[:, 3][None], 'region', axis=0, tiled=True)  81.2 us
    all_gather x1, blocking collectives, body(): lax.all_gather(start_capacity[0], 'tm', axis=0, tiled=True)  61.3 us
    reduce_scatter x4, waiting for transfers between devices, body(): lax.psum_scatter(jnp.einsum('jq,jhk->qhk', own_sources, partial_lines, pr...  60.6 us
    ppermute x20, starting transfers between devices, return_all_array_up(): ppermute(current_value, axis_name=axis_key, perm=[(idx, idx ^ 1 << new) f...  43.7 us
    dot_general x4, matrix products, network_adjoint(): jnp.einsum('hil,iskl->hisk', dual_rows, weights, precision=HIGHEST_PRECIS...  37 us
    dot_general x4, matrix products, network_forward(): jnp.einsum('hpk,pkl->hpl', picked, flat_weights, precision=HIGHEST_PRECIS...  31.7 us
    ppermute x8, starting transfers between devices, shifted(): return lax.ppermute(shard, axis, pairs)  15.1 us
  transfers between devices with their start and end apart: 32, of which 10 were waited for; matrix products, arithmetic and copies ran while one was open for 14% of the time, Pallas kernels for 0%

profile of v1, /device:TPU:1, one launch (start us, length us, event | category | flops | bytes accessed | tf_op | source)
XLA Modules:
  0.0 688.4 jit_solution(3193529362309019845)
XLA Ops:
  9.5 2.7 collective-permute-start.1
  16.5 9.0 %fusion.6 = f32[25,64,3,128]{3,1,2,0:T(8,128)S(1)} fusion(f32[1,25,3,128,128]{4,3,2,1,0:T(8,128)} %param.57), kind=kOutput, calls=%fused_computation.10 | convolution fusion | flops 943718400 | bytes 7372800 | tf_op jit(solution)/shard_map/hil,iskl->hisk/dot_general | solution.py:30
  29.4 3.1 collective-permute-start.2
  37.1 3.0 collective-permute-start.4
  42.1 3.1 reduce.43
  45.2 61.3 %all-reduce.6 = (f32[128]{0:T(128)S(1)}, f32[128]{0:T(128)S(1)}) all-reduce(f32[128]{0:T(128)S(1)} %bitcast_dynamic-update-slice_fusion.1, f32[128]{0:T(128)S(1)} %bitcast_dynamic-update-slice_fusion), channel_id=2, replica_groups=mesh['tm'=32,'region'=8] {'tm'}, use_global_device_ids=true, to_apply=%add.1 | all-reduce | flops 256 | bytes 2048 | tf_op jit(solution)/shard_map/all_gather | solution.py:76
  108.9 4.0 collective-permute-done.5
  117.1 32.1 %all-gather.2 = f32[512,1,128]{2,1,0:T(1,128)S(1)} all-gather(f32[64,1,128]{2,1,0:T(1,128)S(1)} %bitcast.388), channel_id=4, replica_groups=mesh['tm'=32,'region'=8] {'region'}, dimensions={0}, use_global_device_ids=true | all-gather | bytes 294912 | tf_op jit(solution)/shard_map/all_gather | solution.py:129
  151.3 7.9 %fusion.22 = f32[75,64,128]{2,1,0:T(8,128)} fusion(f32[75,128,128]{2,1,0:T(8,128)} %bitcast.361, f32[75,64,128]{2,1,0:T(8,128)} %gather_fusion, pred[75]{0:T(512)(128)(4,1)S(1)} %compare_and_fusion), kind=kOutput, calls=%fused_computation.26 | convolution fusion | flops 944332800 | bytes 9830475 | tf_op jit(solution)/shard_map/hpk,pkl->hpl/dot_general | solution.py:24
  164.3 9.3 %fusion.4 = f32[25,64,3,128]{3,1,2,0:T(8,128)S(1)} fusion(f32[1,25,3,128,128]{4,3,2,1,0:T(8,128)} %param.57, f32[64,25,128]{2,0,1:T(8,128)S(1)} %get-tuple-element.280), kind=kOutput, calls=%fused_computation.8 | convolution fusion | flops 943718400 | bytes 8192000 | tf_op jit(solution)/shard_map/hil,iskl->hisk/dot_general | solution.py:30
  180.9 79.0 %all-reduce.5 = (f32[]{:T(128)}, f32[]{:T(128)}) all-reduce(f32[]{:T(128)S(6)} %add.306, f32[]{:T(128)} %get-tuple-element.279), channel_id=1, replica_groups=mesh['tm'=32,'region'=8] {'tm','region'}, use_global_device_ids=true, to_apply=%region_3.4 | all-reduce | flops 2 | bytes 16 | tf_op jit(solution)/shard_map/psum | solution.py:122
  273.6 2.8 collective-permute-done.12
  277.3 20.0 %reduce-scatter.7.cloned.1.call-done = f32[1,64,128]{2,1,0:T(8,128)} async-done(((f32[8,64,128]{2,1,0:T(8,128)}), f32[1,64,128]{2,1,0:T(8,128)}) %reduce-scatter.7.cloned.1.call-update) | async-done | bytes 32784 | tf_op jit(solution)/shard_map/reduce_scatter | solution.py:88
  304.0 2.9 collective-permute-start.13
  306.8 16.3 %all-gather.3 = f32[512,1,128]{2,1,0:T(1,128)S(1)} all-gather(f32[64,1,128]{2,1,0:T(1,128)S(1)} %bitcast.386), channel_id=5, replica_groups=mesh['tm'=32,'region'=8] {'region'}, dimensions={0}, use_global_device_ids=true | all-gather | bytes 294912 | tf_op jit(solution)/shard_map/all_gather | solution.py:129
  323.1 7.9 %fusion.20 = f32[75,64,128]{2,1,0:T(8,128)} fusion(f32[75,128,128]{2,1,0:T(8,128)} %bitcast.362, f32[75,64,128]{2,1,0:T(8,128)} %gather_fusion.1, pred[75]{0:T(512)(128)(4,1)S(1)} %compare_and_fusion), kind=kOutput, calls=%fused_computation.24 | convolution fusion | flops 944332800 | bytes 9830475 | tf_op jit(solution)/shard_map/hpk,pkl->hpl/dot_general | solution.py:24
  336.2 9.3 %fusion.2 = f32[25,64,3,128]{3,1,2,0:T(8,128)S(1)} fusion(f32[1,25,3,128,128]{4,3,2,1,0:T(8,128)} %param.57, f32[64,25,128]{2,0,1:T(8,128)S(1)} %get-tuple-element.274), kind=kOutput, calls=%fused_computation.6 | convolution fusion | flops 943718400 | bytes 8192000 | tf_op jit(solution)/shard_map/hil,iskl->hisk/dot_general | solution.py:30
  352.3 2.5 collective-permute-start.16
  358.5 76.9 %all-reduce.4 = (f32[]{:T(128)}, f32[]{:T(128)}) all-reduce(f32[]{:T(128)S(6)} %add.319, f32[]{:T(128)} %get-tuple-element.273), channel_id=1, replica_groups=mesh['tm'=32,'region'=8] {'tm','region'}, use_global_device_ids=true, to_apply=%region_11.13 | all-reduce | flops 2 | bytes 16 | tf_op jit(solution)/shard_map/psum | solution.py:122
  441.5 3.3 collective-permute-start.19
  448.8 20.2 %reduce-scatter.9.cloned.1.call-done = f32[1,64,128]{2,1,0:T(8,128)} async-done(((f32[8,64,128]{2,1,0:T(8,128)}), f32[1,64,128]{2,1,0:T(8,128)}) %reduce-scatter.9.cloned.1.call-update) | async-done | bytes 32784 | tf_op jit(solution)/shard_map/reduce_scatter | solution.py:88
  474.7 2.8 collective-permute-start.20
  477.6 16.6 %all-gather.4 = f32[512,1,128]{2,1,0:T(1,128)S(1)} all-gather(f32[64,1,128]{2,1,0:T(1,128)S(1)} %bitcast.387), channel_id=6, replica_groups=mesh['tm'=32,'region'=8] {'region'}, dimensions={0}, use_global_device_ids=true | all-gather | bytes 294912 | tf_op jit(solution)/shard_map/all_gather | solution.py:129
  494.1 7.9 %fusion.18 = f32[75,64,128]{2,1,0:T(8,128)} fusion(f32[75,128,128]{2,1,0:T(8,128)} %bitcast.363, f32[75,64,128]{2,1,0:T(8,128)} %gather_fusion.2, pred[75]{0:T(512)(128)(4,1)S(1)} %compare_and_fusion), kind=kOutput, calls=%fused_computation.22 | convolution fusion | flops 944332800 | bytes 9830475 | tf_op jit(solution)/shard_map/hpk,pkl->hpl/dot_general | solution.py:24
  508.3 9.3 %fusion = f32[25,64,3,128]{3,1,2,0:T(8,128)S(1)} fusion(f32[1,25,3,128,128]{4,3,2,1,0:T(8,128)} %param.57, f32[64,25,128]{2,0,1:T(8,128)S(1)} %get-tuple-element.270), kind=kOutput, calls=%fused_computation.4 | convolution fusion | flops 943718400 | bytes 8192000 | tf_op jit(solution)/shard_map/hil,iskl->hisk/dot_general | solution.py:30
  530.6 76.9 %all-reduce.3 = (f32[]{:T(128)}, f32[]{:T(128)}) all-reduce(f32[]{:T(128)S(6)} %add.333, f32[]{:T(128)} %get-tuple-element.269), channel_id=1, replica_groups=mesh['tm'=32,'region'=8] {'tm','region'}, use_global_device_ids=true, to_apply=%region_19.21 | all-reduce | flops 2 | bytes 16 | tf_op jit(solution)/shard_map/psum | solution.py:122
  613.4 3.3 collective-permute-start.27
  620.6 20.4 %reduce-scatter.11.cloned.1.call-done = f32[1,64,128]{2,1,0:T(8,128)} async-done(((f32[8,64,128]{2,1,0:T(8,128)}), f32[1,64,128]{2,1,0:T(8,128)}) %reduce-scatter.11.cloned.1.call-update) | async-done | bytes 32784 | tf_op jit(solution)/shard_map/reduce_scatter | solution.py:88
  642.4 2.7 multiply_subtract_fusion
  647.2 2.8 collective-permute-start.22
  650.0 16.3 %all-gather.5 = f32[512,1,128]{2,1,0:T(1,128)S(1)} all-gather(f32[64,1,128]{2,1,0:T(1,128)S(1)} %bitcast.385), channel_id=7, replica_groups=mesh['tm'=32,'region'=8] {'region'}, dimensions={0}, use_global_device_ids=true | all-gather | bytes 294912 | tf_op jit(solution)/shard_map/all_gather | solution.py:129
  666.3 8.0 %fusion.16 = f32[75,64,128]{2,1,0:T(8,128)} fusion(f32[75,128,128]{2,1,0:T(8,128)} %bitcast.364, f32[75,64,128]{2,1,0:T(8,128)} %gather_fusion.3, pred[75]{0:T(512)(128)(4,1)S(1)} %compare_and_fusion), kind=kOutput, calls=%fused_computation.20 | convolution fusion | flops 944332800 | bytes 9830475 | tf_op jit(solution)/shard_map/hpk,pkl->hpl/dot_general | solution.py:24
  (227 shorter events, 121.2 us)
Async XLA Ops:
  7.2 106.6 %reduce-scatter.5.cloned.1.call-start = ((), (), s32[]{:S(2)}) async-start(), calls=%async_computation.4 | async-start | bytes 294912 | tf_op jit(solution)/shard_map/reduce_scatter | solution.py:88
  7.2 101.6 %collective-permute-start = (f32[128]{0:T(128)S(1)}, f32[128]{0:T(128)S(1)}, u32[]{:S(2)}, u32[]{:S(2)}) collective-permute-start(f32[128]{0:T(128)S(1)} %broadcast.305), channel_id=1, source_target_pairs={{8,0},{16,8},{24,16},{32,24},{40,32},{48,40},{56,48},{64,56},{72,6... | collective-permute-start | bytes 1544 | tf_op jit(solution)/shard_map/ppermute | solution.py:17
  9.5 19.9 %collective-permute-start.1 = (f32[128]{0:T(128)S(1)}, f32[128]{0:T(128)S(1)}, u32[]{:S(2)}, u32[]{:S(2)}) collective-permute-start(f32[128]{0:T(128)S(1)} %fusion.51), channel_id=1, source_target_pairs={{0,8},{8,0},{16,24},{24,16},{32,40},{40,32},{48,56},{56,48},{64,72... | collective-permute-start | bytes 1544 | tf_op jit(solution)/shard_map/ppermute | solution.py:104
  15.5 281.9 %reduce-scatter.7.cloned.1.call-start = ((), (), s32[]{:S(2)}) async-start(), calls=%async_computation.5 | async-start | bytes 294912 | tf_op jit(solution)/shard_map/reduce_scatter | solution.py:88
  29.4 4.1 collective-permute-start.2
  33.5 3.6 collective-permute-start.3
  37.1 69.4 %collective-permute-start.4 = (f32[128]{0:T(128)S(1)}, f32[128]{0:T(128)S(1)}, u32[]{:S(2)}, u32[]{:S(2)}) collective-permute-start(f32[128]{0:T(128)S(1)} %add.302), channel_id=1, source_target_pairs={{0,64},{8,72},{16,80},{24,88},{32,96},{40,104},{48,112},{56,120},{... | collective-permute-start | bytes 1544 | tf_op jit(solution)/shard_map/ppermute | solution.py:104
  106.5 6.4 collective-permute-start.5
  115.8 47.2 %collective-permute-start.6 = (f32[128]{0:T(128)S(1)}, f32[128]{0:T(128)S(1)}, u32[]{:S(2)}, u32[]{:S(2)}) collective-permute-start(f32[128]{0:T(128)S(1)} %slice_bitcast_fusion.16), channel_id=1, source_target_pairs={{0,8},{8,16},{16,24},{24,32},{32,40},{40,48},{48,56},{56,64},{64,7... | collective-permute-start | bytes 1544 | tf_op jit(solution)/shard_map/ppermute | solution.py:17
  173.8 98.4 %collective-permute-start.7 = (f32[128]{0:T(128)S(1)}, f32[128]{0:T(128)S(1)}, u32[]{:S(2)}, u32[]{:S(2)}) collective-permute-start(f32[128]{0:T(128)S(1)} %slice_bitcast_fusion.15), channel_id=1, source_target_pairs={{8,0},{16,8},{24,16},{32,24},{40,32},{48,40},{56,48},{64,56},{72,6... | collective-permute-start | bytes 1544 | tf_op jit(solution)/shard_map/ppermute | solution.py:17
  175.2 5.2 collective-permute-start.8
  180.4 79.5 %collective-permute-start.9 = (f32[128]{0:T(128)S(1)}, f32[128]{0:T(128)S(1)}, u32[]{:S(2)}, u32[]{:S(2)}) collective-permute-start(f32[128]{0:T(128)S(1)} %add.314), channel_id=1, source_target_pairs={{0,16},{8,24},{16,0},{24,8},{32,48},{40,56},{48,32},{56,40},{64,80... | collective-permute-start | bytes 1544 | tf_op jit(solution)/shard_map/ppermute | solution.py:104
  259.9 3.2 collective-permute-start.10
  263.2 6.9 collective-permute-start.11
  270.0 199.0 %reduce-scatter.9.cloned.1.call-start = ((), (), s32[]{:S(2)}) async-start(), calls=%async_computation.6 | async-start | bytes 294912 | tf_op jit(solution)/shard_map/reduce_scatter | solution.py:88
  270.1 6.4 collective-permute-start.12
  304.0 30.8 %collective-permute-start.13 = (f32[128]{0:T(128)S(1)}, f32[128]{0:T(128)S(1)}, u32[]{:S(2)}, u32[]{:S(2)}) collective-permute-start(f32[128]{0:T(128)S(1)} %slice_bitcast_fusion.14), channel_id=1, source_target_pairs={{0,8},{8,16},{16,24},{24,32},{32,40},{40,48},{48,56},{56,64},{64,7... | collective-permute-start | bytes 1544 | tf_op jit(solution)/shard_map/ppermute | solution.py:17
  345.7 99.1 %collective-permute-start.14 = (f32[128]{0:T(128)S(1)}, f32[128]{0:T(128)S(1)}, u32[]{:S(2)}, u32[]{:S(2)}) collective-permute-start(f32[128]{0:T(128)S(1)} %slice_bitcast_fusion.13), channel_id=1, source_target_pairs={{8,0},{16,8},{24,16},{32,24},{40,32},{48,40},{56,48},{64,56},{72,6... | collective-permute-start | bytes 1544 | tf_op jit(solution)/shard_map/ppermute | solution.py:17
  347.0 5.2 collective-permute-start.15
  352.3 4.0 collective-permute-start.16
  356.3 80.5 %collective-permute-start.17 = (f32[128]{0:T(128)S(1)}, f32[128]{0:T(128)S(1)}, u32[]{:S(2)}, u32[]{:S(2)}) collective-permute-start(f32[128]{0:T(128)S(1)} %add.329), channel_id=1, source_target_pairs={{0,32},{8,40},{16,48},{24,56},{32,0},{40,8},{48,16},{56,24},{64,96... | collective-permute-start | bytes 1544 | tf_op jit(solution)/shard_map/ppermute | solution.py:104
  436.8 4.6 collective-permute-start.18
  441.4 199.6 %reduce-scatter.11.cloned.1.call-start = ((), (), s32[]{:S(2)}) async-start(), calls=%async_computation.7 | async-start | bytes 294912 | tf_op jit(solution)/shard_map/reduce_scatter | solution.py:88
  441.5 6.4 collective-permute-start.19
  474.7 31.0 %collective-permute-start.20 = (f32[128]{0:T(128)S(1)}, f32[128]{0:T(128)S(1)}, u32[]{:S(2)}, u32[]{:S(2)}) collective-permute-start(f32[128]{0:T(128)S(1)} %slice_bitcast_fusion.12), channel_id=1, source_target_pairs={{0,8},{8,16},{16,24},{24,32},{32,40},{40,48},{48,56},{56,64},{64,7... | collective-permute-start | bytes 1544 | tf_op jit(solution)/shard_map/ppermute | solution.py:17
  517.8 98.9 %collective-permute-start.21 = (f32[128]{0:T(128)S(1)}, f32[128]{0:T(128)S(1)}, u32[]{:S(2)}, u32[]{:S(2)}) collective-permute-start(f32[128]{0:T(128)S(1)} %slice_bitcast_fusion.11), channel_id=1, source_target_pairs={{8,0},{16,8},{24,16},{32,24},{40,32},{48,40},{56,48},{64,56},{72,6... | collective-permute-start | bytes 1544 | tf_op jit(solution)/shard_map/ppermute | solution.py:17
  519.1 5.2 collective-permute-start.23
  524.3 4.0 collective-permute-start.24
  528.3 80.5 %collective-permute-start.25 = (f32[128]{0:T(128)S(1)}, f32[128]{0:T(128)S(1)}, u32[]{:S(2)}, u32[]{:S(2)}) collective-permute-start(f32[128]{0:T(128)S(1)} %add.345), channel_id=1, source_target_pairs={{0,32},{8,40},{16,48},{24,56},{32,0},{40,8},{48,16},{56,24},{64,96... | collective-permute-start | bytes 1544 | tf_op jit(solution)/shard_map/ppermute | solution.py:104
  608.9 4.6 collective-permute-start.26
  613.4 6.4 collective-permute-start.27
  647.2 31.8 %collective-permute-start.22 = (f32[128]{0:T(128)S(1)}, f32[128]{0:T(128)S(1)}, u32[]{:S(2)}, u32[]{:S(2)}) collective-permute-start(f32[128]{0:T(128)S(1)} %slice_bitcast_fusion.10), channel_id=1, source_target_pairs={{0,8},{8,16},{16,24},{24,32},{32,40},{40,48},{48,56},{56,64},{64,7... | collective-permute-start | bytes 1544 | tf_op jit(solution)/shard_map/ppermute | solution.py:17
  (17 other events, 413.6 us)
Sparse Core Ops, SparseCore 0:
  15.6 35.0 reduce-scatter.4
  270.1 27.2 reduce-scatter.6
  441.5 27.4 reduce-scatter.8
  613.5 27.4 reduce-scatter.10
